TPU v7x, 32 devices: a whole 2x2x4 slice. The times are simulated.
32 devices in a mesh: groups: 2 (over y), mem: 4 (over z), head: 2 (over x), width: 2 (over core).
Axes of the slice: x: 2, y: 2, z: 4, core: 2. Of those that a mesh axis runs over, the one named last changes fastest.
Arguments:
- residual_in: bfloat16 [64, 5120], P('groups', 'mem'), parts along dimension 0, may hold values from -26 to 26
- attention_gain: float32 [5120], P('mem'), may hold values from 0.5 to 1.5
- query_weight: bfloat16 [5120, 8192], P('mem', ('head', 'width')), may hold values from -0.078125 to 0.078125
- key_weight: bfloat16 [5120, 1024], P('mem', ('head', 'width')), may hold values from -0.078125 to 0.078125
- value_weight: bfloat16 [5120, 1024], P('mem', ('head', 'width')), may hold values from -0.078125 to 0.078125
- query_norm: float32 [128], replicated, may hold values from 0.25 to 1.75
- key_norm: float32 [128], replicated, may hold values from 0.1 to 1.9
- cache_keys: bfloat16 [65536, 8, 128], P(('groups', 'mem'), ('head', 'width')), parts along dimension 0, may hold values from -480 to 480
- cache_values: bfloat16 [65536, 8, 128], P(('groups', 'mem'), ('head', 'width')), parts along dimension 0, may hold values from -12 to 12
- slot_request: int32 [65536], P(('groups', 'mem')), parts along dimension 0, may hold values from 0 to 16, as said below
- lengths: int32 [32], P('groups'), parts along dimension 0, may hold values from 1056 to 1760, as said below
- output_weight: bfloat16 [8192, 5120], P(('head', 'width'), 'mem'), may hold values from -0.0625 to 0.0625
- second_gain: float32 [5120], P('mem'), may hold values from 0.5 to 1.5
- gate_weight: bfloat16 [5120, 25600], P('mem', ('head', 'width')), may hold values from -0.078125 to 0.078125
- up_weight: bfloat16 [5120, 25600], P('mem', ('head', 'width')), may hold values from -0.078125 to 0.078125
- down_weight: bfloat16 [25600, 5120], P(('head', 'width'), 'mem'), may hold values from -0.0390625 to 0.0390625
Outputs:
- layer_out: bfloat16 [64, 5120], P('groups', 'mem'), parts along dimension 0
There are 2 independent parts, one for each index of `groups`. A program takes and returns all parts, laid end to end along the dimension named above; an argument that names none is the same for every part. Nothing has to cross between parts.
Inputs may be any that keep to these rules, and one draw needn't show every extreme that they name: slot_request[s] names the request whose cached token sits in slot s, or is 16 for an empty slot. On each owner (each aligned block of 8192 slots along mem) the used slots come first; taking owners in order and their used slots in order, requests 0 to 15 follow one another in consecutive slots, so a request may continue on the next owner, but on no further one: a request's slots lie on at most two consecutive owners. Request r has exactly lengths[r] slots. Some owner has all its slots used. lengths[r] is the number of cached tokens of request r; its new tokens stand at positions lengths[r] and lengths[r] + 1.
All inputs are finite; a program needn't handle non-finite values.
Results may differ from a plain program's by a relative error of at most 0.0095.
The roundings to bfloat16 on the way count: a program that leaves them out, or rounds other values in their place, can miss the bound.
Values may be sent and summed in bfloat16 or wider, within the bound.
A program may use at most 128 MiB of HBM per device.

v0:
```python
import math
import jax
import jax.numpy as jnp
from jax import lax
from jax.sharding import PartitionSpec as P

D = 5120
epsilon = 1e-06
rope_base = 1000000.0
floor_score = -1e30


def combined_all(value, axis, join):
    pieces = jax.tree.map(lambda part: lax.all_gather(part, axis), value)
    head = jax.tree.map(lambda part: part[0], pieces)
    tail = jax.tree.map(lambda part: part[1:], pieces)
    running, _ = lax.scan(lambda running, slab: (join(running, slab), None), head, tail)
    return running


def rotate(values, places):
    breadth = values.shape[-1]
    halfway = breadth // 2
    frequency = rope_base ** (-(jnp.arange(halfway, dtype=jnp.float32) * 2.0) / breadth)
    angles = places[..., None] * frequency
    cosine = jnp.cos(angles)
    sine_part = jnp.sin(angles)
    leading = values[..., :halfway]
    trailing = values[..., halfway:]
    return jnp.concatenate(
        [leading * cosine - trailing * sine_part, trailing * cosine + leading * sine_part], axis=-1
    )


def head_norm(values, scaling):
    mean_square = jnp.mean(values * values, axis=-1, keepdims=True)
    return values * lax.rsqrt(mean_square + epsilon) * scaling


def combine(first, second):
    first_top, first_sum, first_acc = first
    second_top, second_sum, second_acc = second
    highest = jnp.maximum(first_top, second_top)
    first_factor = jnp.exp(first_top - highest)
    second_factor = jnp.exp(second_top - highest)
    return (
        highest,
        first_sum * first_factor + second_sum * second_factor,
        first_acc * first_factor[..., None] + second_acc * second_factor[..., None],
    )


def per_device(
    residual_in,
    attention_gain,
    query_weight,
    key_weight,
    value_weight,
    query_norm,
    key_norm,
    cache_keys,
    cache_values,
    slot_request,
    lengths,
    output_weight,
    second_gain,
    gate_weight,
    up_weight,
    down_weight,
):
    row_count = residual_in.shape[0]
    requests = row_count // 2
    head_dim = query_norm.shape[0]
    kv_here = cache_keys.shape[1]
    q_here = query_weight.shape[1] // head_dim
    group_size = q_here // kv_here
    score_scale = 1.0 / math.sqrt(head_dim)
    residual = residual_in.astype(jnp.float32)
    squares = lax.psum(jnp.sum(residual * residual, axis=1), "mem")
    normed = (residual * lax.rsqrt(squares / D + epsilon)[:, None] * attention_gain).astype(
        jnp.bfloat16
    )
    query_part = jnp.dot(normed, query_weight, preferred_element_type=jnp.float32)
    key_part = jnp.dot(normed, key_weight, preferred_element_type=jnp.float32)
    value_part = jnp.dot(normed, value_weight, preferred_element_type=jnp.float32)
    offsets = jnp.arange(2, dtype=jnp.int32)
    places = (lengths[:, None] + offsets[None, :]).reshape(row_count).astype(jnp.float32)
    query_sum, key_sum, value_sum = lax.psum((query_part, key_part, value_part), "mem")
    count_rows = query_sum.shape[0]
    query_rot = rotate(
        head_norm(query_sum.reshape(count_rows, q_here, head_dim), query_norm), places[:, None]
    )
    key_rot = rotate(
        head_norm(key_sum.reshape(count_rows, kv_here, head_dim), key_norm), places[:, None]
    )
    queries = query_rot.astype(jnp.bfloat16)
    new_keys = key_rot.astype(jnp.bfloat16)
    new_values = value_sum.reshape(count_rows, kv_here, head_dim).astype(jnp.bfloat16)
    queries_split = queries.reshape(row_count, kv_here, group_size, head_dim)
    row_owner = jnp.arange(row_count, dtype=jnp.int32) // 2
    capacity = cache_keys.shape[0]
    block_size = min(1024, capacity)
    used_slots = jnp.sum((slot_request < requests).astype(jnp.int32))
    used_blocks = (used_slots + block_size - 1) // block_size
    start_state = (
        jnp.full((row_count, kv_here, group_size), floor_score, jnp.float32),
        jnp.zeros((row_count, kv_here, group_size), jnp.float32),
        jnp.zeros((row_count, kv_here, group_size, head_dim), jnp.float32),
    )

    def visit_block(counter, carried):
        highest, summed, running = carried
        first_slot = counter * block_size
        key_block = lax.dynamic_slice_in_dim(cache_keys, first_slot, block_size, 0)
        value_block = lax.dynamic_slice_in_dim(cache_values, first_slot, block_size, 0)
        owner_block = lax.dynamic_slice_in_dim(slot_request, first_slot, block_size, 0)
        scores = (
            jnp.einsum(
                "bkgd,skd->bkgs", queries_split, key_block, preferred_element_type=jnp.float32
            )
            * score_scale
        )
        matches = (owner_block[None, :] == row_owner[:, None])[:, None, None, :]
        block_top = jnp.max(jnp.where(matches, scores, floor_score), axis=-1)
        updated = jnp.maximum(highest, block_top)
        weights = jnp.where(matches, jnp.exp(scores - updated[..., None]), 0.0)
        factor = jnp.exp(highest - updated)
        summed = summed * factor + jnp.sum(weights, axis=-1)
        running = running * factor[..., None] + jnp.einsum(
            "bkgs,skd->bkgd",
            weights.astype(jnp.bfloat16),
            value_block,
            preferred_element_type=jnp.float32,
        )
        return (updated, summed, running)

    highest, summed, running = lax.fori_loop(0, used_blocks, visit_block, start_state)
    highest, summed, running = combined_all((highest, summed, running), "mem", combine)
    query_pairs = queries.reshape(requests, 2, kv_here, group_size, head_dim)
    key_pairs = new_keys.reshape(requests, 2, kv_here, head_dim)
    value_pairs = new_values.reshape(requests, 2, kv_here, head_dim)
    allowed = (offsets[None, :] <= offsets[:, None])[None, :, None, None, :]
    allowed_rows = jnp.broadcast_to(allowed, (requests, 2, kv_here, group_size, 2)).reshape(
        row_count, kv_here, group_size, 2
    )
    own_scores = (
        jnp.einsum("rtkgd,rskd->rtkgs", query_pairs, key_pairs, preferred_element_type=jnp.float32)
        * score_scale
    )
    own_scores = jnp.where(allowed, own_scores, floor_score).reshape(
        row_count, kv_here, group_size, 2
    )
    final_top = jnp.maximum(highest, jnp.max(own_scores, axis=-1))
    own_weights = jnp.where(allowed_rows, jnp.exp(own_scores - final_top[..., None]), 0.0)
    factor = jnp.exp(highest - final_top)
    summed = summed * factor + jnp.sum(own_weights, axis=-1)
    own_rounded = own_weights.astype(jnp.bfloat16).reshape(requests, 2, kv_here, group_size, 2)
    own_values = jnp.einsum(
        "rtkgs,rskd->rtkgd", own_rounded, value_pairs, preferred_element_type=jnp.float32
    )
    running = running * factor[..., None] + own_values.reshape(
        row_count, kv_here, group_size, head_dim
    )
    attended = (
        (running / summed[..., None]).reshape(row_count, q_here * head_dim).astype(jnp.bfloat16)
    )
    projected = lax.psum(
        jnp.dot(attended, output_weight, preferred_element_type=jnp.float32), ("head", "width")
    )
    middle = (residual + projected).astype(jnp.bfloat16)
    middle_wide = middle.astype(jnp.float32)
    squares_mid = lax.psum(jnp.sum(middle_wide * middle_wide, axis=1), "mem")
    normed_mid = (middle_wide * lax.rsqrt(squares_mid / D + epsilon)[:, None] * second_gain).astype(
        jnp.bfloat16
    )
    gate_part = jnp.dot(normed_mid, gate_weight, preferred_element_type=jnp.float32)
    up_part = jnp.dot(normed_mid, up_weight, preferred_element_type=jnp.float32)
    gate_sum, up_sum = (
        lax.psum_scatter(gate_part, "mem", scatter_dimension=0, tiled=True),
        lax.psum_scatter(up_part, "mem", scatter_dimension=0, tiled=True),
    )
    activated = lax.all_gather(
        (jax.nn.silu(gate_sum) * up_sum).astype(jnp.bfloat16), "mem", axis=0, tiled=True
    )
    down_sum = lax.psum(
        jnp.dot(activated, down_weight, preferred_element_type=jnp.float32), ("head", "width")
    )
    return (middle_wide + down_sum).astype(jnp.bfloat16)


def solution(mesh):
    return jax.shard_map(
        per_device,
        mesh=mesh,
        in_specs=(
            P("groups", "mem"),
            P("mem"),
            P("mem", ("head", "width")),
            P("mem", ("head", "width")),
            P("mem", ("head", "width")),
            P(),
            P(),
            P(("groups", "mem"), ("head", "width"), None),
            P(("groups", "mem"), ("head", "width"), None),
            P(("groups", "mem")),
            P("groups"),
            P(("head", "width"), "mem"),
            P("mem"),
            P("mem", ("head", "width")),
            P("mem", ("head", "width")),
            P(("head", "width"), "mem"),
        ),
        out_specs=P("groups", "mem"),
        check_vma=False,
    )
```

profile of v0, /device:TPU:0, one launch (start us, length us, event | category | flops | bytes accessed | tf_op | source)
XLA Modules:
  0.0 318.0 jit_solution(10210930667824503828)
XLA Ops:
  6.6 1.1 fusion.24
  7.7 13.5 %psum.49 = f32[32]{0:T(128)S(1)} all-reduce(f32[32]{0:T(128)S(1)} %fusion.24), channel_id=1, replica_groups=mesh['groups'=2,'mem'=4,'head'=2,'width'=2] {'mem'}, use_global_device_ids=true, to_apply=%region_2.0 | all-reduce | flops 32 | bytes 256 | tf_op jit(solution)/shard_map/psum | solution.py:79
  21.1 3.6 %convolution_bitcast_fusion.1 = f32[4,8,16,128]{3,1,2,0:T(8,128)S(1)} fusion(bf16[1280,2048]{1,0:T(8,128)(2,1)} %param.22, bf16[32,1280]{1,0:T(8,128)(2,1)} %param.20, f32[1280]{0:T(1024)} %param.21, f32[32]{0:T(128)S(1)} %add_rsqrt_fusion.3), kind=kOutput, calls=%fused_computation.38 | convolution fusion | flops 167936000 | bytes 5592192 | tf_op jit(solution)/shard_map/dot_general | solution.py:83
  24.7 0.8 copy.134
  25.6 0.7 convert_reduce_fusion
  27.3 32.1 %all-reduce.5.cloned.1.call-done = f32[32,16,128]{2,1,0:T(8,128)} async-done(((f32[32,16,128]{2,1,0:T(8,128)}), f32[32,16,128]{2,1,0:T(8,128)}) %all-reduce.5.cloned.1.call-update) | async-done | bytes 262160 | tf_op jit(solution)/shard_map/psum | solution.py:88
  59.5 1.1 multiply_reduce_fusion
  60.6 1.1 multiply_multiply_fusion
  62.2 12.0 %while.30 = (s32[]{:T(128)}, f32[32,2,8]{0,2,1:T(8,128)S(1)}, f32[32,2,8]{0,2,1:T(8,128)S(1)}, f32[32,2,8,128]{3,0,2,1:T(8,128)S(1)}, s32[]{:T(128)}, /*index=5*...) while((s32[]{:T(128)}, f32[32,2,8]{0,2,1:T(8,128)S(1)}, ...), condition=%wide.region_8.9_spmd.clone, body=%wide.region_5.8_spmd.clone.sunk | while | flops 274367744 | bytes 10269107 | solution.py:137
  62.3 2.0 constant_dynamic-slice_fusion.6
  66.3 1.9 constant_dynamic-slice_fusion.6
  70.3 1.9 constant_dynamic-slice_fusion.6
  75.5 39.0 %all-reduce = (bf16[32,256]{1,0:T(8,128)(2,1)S(1)}, f32[32,2,128]{2,0,1:T(8,128)S(1)}) all-reduce(f32[32,256]{1,0:T(8,128)S(1)} %fusion.45, f32[32,2,128]{2,0,1:T(8,128)S(1)} %bitcast.129), channel_id=1, replica_groups=mesh['groups'=2,'mem'=4,'head'=2,'width'=2] {'mem'}, use_global_device_ids=true, to_apply=%region_14.15 | all-reduce | flops 16384 | bytes 114688 | tf_op jit(solution)/shard_map/psum | solution.py:88
  114.9 14.1 %all-gather.1 = f32[128,2,8]{2,1,0:T(2,128)S(1)} all-gather(f32[32,2,8]{2,1,0:T(2,128)S(1)} %copy.92), channel_id=3, replica_groups=mesh['groups'=2,'mem'=4,'head'=2,'width'=2] {'mem'}, dimensions={0}, use_global_device_ids=true | all-gather | bytes 10240 | tf_op jit(solution)/shard_map/all_gather | solution.py:14
  129.0 13.3 %all-gather = f32[128,2,8]{2,1,0:T(2,128)S(1)} all-gather(f32[32,2,8]{2,1,0:T(2,128)S(1)} %copy.91), channel_id=2, replica_groups=mesh['groups'=2,'mem'=4,'head'=2,'width'=2] {'mem'}, dimensions={0}, use_global_device_ids=true | all-gather | bytes 10240 | tf_op jit(solution)/shard_map/all_gather | solution.py:14
  142.4 0.8 fusion.51
  143.6 1.0 slice.50
  144.8 1.2 slice.53
  146.0 1.7 while.29
  148.8 4.1 %fusion.32 = f32[32,1280]{1,0:T(8,128)} fusion(bf16[2048,1280]{1,0:T(8,128)(2,1)} %param.31, bf16[4,8,16,128]{3,2,1,0:T(8,128)(2,1)S(1)} %bitcast.122), kind=kOutput, calls=%fused_computation.66 | convolution fusion | flops 167772160 | bytes 5537792 | tf_op jit(solution)/shard_map/dot_general | solution.py:168
  152.9 31.2 %all-reduce.7.cloned.1.call-done = f32[32,1280]{1,0:T(8,128)} async-done(((f32[32,1280]{1,0:T(8,128)}), f32[32,1280]{1,0:T(8,128)}) %all-reduce.7.cloned.1.call-update) | async-done | bytes 163856 | tf_op jit(solution)/shard_map/psum | solution.py:167
  184.1 1.0 fusion.28
  185.1 11.7 %psum.54 = f32[32]{0:T(128)S(1)} all-reduce(f32[32]{0:T(128)S(1)} %get-tuple-element.230), channel_id=1, replica_groups=mesh['groups'=2,'mem'=4,'head'=2,'width'=2] {'mem'}, use_global_device_ids=true, to_apply=%region_18.19 | all-reduce | flops 32 | bytes 256 | tf_op jit(solution)/shard_map/psum | solution.py:172
  196.8 9.6 %fusion.37 = f32[32,6400]{1,0:T(8,128)} fusion(bf16[1280,6400]{1,0:T(8,128)(2,1)} %param.34, bf16[32,1280]{1,0:T(8,128)(2,1)S(1)} %get-tuple-element.231, f32[1280]{0:T(1024)S(1)} %copy-done.5, f32[32]{0:T(128)S(1)} %add_rsqrt_fusion.2), kind=kOutput, calls=%fused_computation.82 | convolution fusion | flops 524451840 | bytes 17290368 | tf_op jit(solution)/shard_map/dot_general | solution.py:177
  206.7 9.7 %fusion.39 = f32[32,6400]{1,0:T(8,128)} fusion(bf16[1280,6400]{1,0:T(8,128)(2,1)} %param.33, bf16[32,1280]{1,0:T(8,128)(2,1)S(1)} %get-tuple-element.231, f32[1280]{0:T(1024)S(1)} %copy-done.5, f32[32]{0:T(128)S(1)} %add_rsqrt_fusion.2), kind=kOutput, calls=%fused_computation.83 | convolution fusion | flops 524451840 | bytes 17290368 | tf_op jit(solution)/shard_map/dot_general | solution.py:176
  216.5 11.0 %reduce-scatter.5.cloned.1.call-done = f32[8,6400]{1,0:T(8,128)} async-done(((f32[32,6400]{1,0:T(8,128)}), f32[8,6400]{1,0:T(8,128)}) %reduce-scatter.5.cloned.1.call-update) | async-done | bytes 204816 | tf_op jit(solution)/shard_map/reduce_scatter | solution.py:180
  227.5 25.2 %reduce-scatter.3.cloned.1.call-done = f32[8,6400]{1,0:T(8,128)} async-done(((f32[32,6400]{1,0:T(8,128)}), f32[8,6400]{1,0:T(8,128)}) %reduce-scatter.3.cloned.1.call-update) | async-done | bytes 204816 | tf_op jit(solution)/shard_map/reduce_scatter | solution.py:179
  252.7 1.1 multiply_convert_fusion
  253.8 15.2 %all_gather.27 = bf16[32,6400]{1,0:T(8,128)(2,1)S(1)} all-gather(bf16[8,6400]{1,0:T(8,128)(2,1)S(1)} %multiply_convert_fusion), channel_id=1, replica_groups=mesh['groups'=2,'mem'=4,'head'=2,'width'=2] {'mem'}, dimensions={0}, use_global_device_ids=true | all-gather | bytes 512000 | tf_op jit(solution)/shard_map/all_gather | solution.py:182
  269.0 9.3 %fusion.52 = f32[32,1280]{1,0:T(8,128)} fusion(bf16[32,6400]{1,0:T(8,128)(2,1)S(1)} %all_gather.27, bf16[6400,1280]{1,0:T(8,128)(2,1)} %param.35), kind=kOutput, calls=%fused_computation.100 | convolution fusion | flops 524288000 | bytes 16957440 | tf_op jit(solution)/shard_map/dot_general | solution.py:186
  278.3 31.2 %all-reduce.9.cloned.1.call-done = f32[32,1280]{1,0:T(8,128)} async-done(((f32[32,1280]{1,0:T(8,128)}), f32[32,1280]{1,0:T(8,128)}) %all-reduce.9.cloned.1.call-update) | async-done | bytes 163856 | tf_op jit(solution)/shard_map/psum | solution.py:185
  309.5 1.6 fusion.31
  (124 shorter events, 12.0 us)
Async XLA Ops:
  6.5 68.4 %copy-start = (bf16[1280,256]{1,0:T(8,128)(2,1)S(1)}, bf16[1280,256]{1,0:T(8,128)(2,1)}, u32[]{:S(2)}) copy-start(bf16[1280,256]{1,0:T(8,128)(2,1)} %param.23) | copy-start | bytes 1966084
  6.5 19.0 %copy-start.6 = (s32[8192]{0:T(1024)S(1)}, s32[8192]{0:T(1024)}, u32[]{:S(2)}) copy-start(s32[8192]{0:T(1024)} %param.29) | copy-start | bytes 98308
  6.5 19.8 %copy-start.10 = (s32[16]{0:T(128)S(1)}, s32[16]{0:T(128)}, u32[]{:S(2)}) copy-start(s32[16]{0:T(128)} %param.30) | copy-start | bytes 196
  6.5 54.0 %copy-start.8 = (f32[128]{0:T(128)S(1)}, f32[128]{0:T(128)}, u32[]{:S(2)}) copy-start(f32[128]{0:T(128)} %param.25) | copy-start | bytes 1540
  6.5 52.9 %all-reduce.5.cloned.1.call-start = ((), (), s32[]{:S(2)}) async-start(), calls=%async_computation.2 | async-start | bytes 524288 | tf_op jit(solution)/shard_map/psum | solution.py:88
  25.5 118.1 %all-gather.5.cloned.1.call-start = ((), (), s32[]{:S(2)}) async-start(), calls=%async_computation.7 | async-start | bytes 1310720 | tf_op jit(solution)/shard_map/all_gather | solution.py:14
  62.1 12.8 %copy-start.2 = (bf16[32,1280]{1,0:T(8,128)(2,1)S(1)}, bf16[32,1280]{1,0:T(8,128)(2,1)}, u32[]{:S(2)}) copy-start(bf16[32,1280]{1,0:T(8,128)(2,1)} %param.20) | copy-start | bytes 245764
  62.1 12.8 %copy-start.7 = (f32[1280]{0:T(1024)S(1)}, f32[1280]{0:T(1024)}, u32[]{:S(2)}) copy-start(f32[1280]{0:T(1024)} %param.21) | copy-start | bytes 15364
  62.1 13.1 %copy-start.4 = (bf16[1280,256]{1,0:T(8,128)(2,1)S(1)}, bf16[1280,256]{1,0:T(8,128)(2,1)}, u32[]{:S(2)}) copy-start(bf16[1280,256]{1,0:T(8,128)(2,1)} %param.24) | copy-start | bytes 1966084
  62.2 52.4 %copy-start.9 = (f32[128]{0:T(128)S(1)}, f32[128]{0:T(128)}, u32[]{:S(2)}) copy-start(f32[128]{0:T(128)} %param.26) | copy-start | bytes 1540
  74.1 0.7 copy-start.3
  74.9 109.2 %all-reduce.7.cloned.1.call-start = ((), (), s32[]{:S(2)}) async-start(), calls=%async_computation.3 | async-start | bytes 327680 | tf_op jit(solution)/shard_map/psum | solution.py:167
  147.6 49.2 %copy-start.5 = (f32[1280]{0:T(1024)S(1)}, f32[1280]{0:T(1024)}, u32[]{:S(2)}) copy-start(f32[1280]{0:T(1024)} %param.32) | copy-start | bytes 15364
  152.9 74.6 %reduce-scatter.5.cloned.1.call-start = ((), (), s32[]{:S(2)}) async-start(), calls=%async_computation.5 | async-start | bytes 1024000 | tf_op jit(solution)/shard_map/reduce_scatter | solution.py:180
  206.4 46.3 %reduce-scatter.3.cloned.1.call-start = ((), (), s32[]{:S(2)}) async-start(), calls=%async_computation.4 | async-start | bytes 1024000 | tf_op jit(solution)/shard_map/reduce_scatter | solution.py:179
  216.4 93.1 %all-reduce.9.cloned.1.call-start = ((), (), s32[]{:S(2)}) async-start(), calls=%async_computation.6 | async-start | bytes 327680 | tf_op jit(solution)/shard_map/psum | solution.py:185
  269.0 42.1 %copy-start.1 = (bf16[1280,256]{1,0:T(8,128)(2,1)S(1)}, bf16[1280,256]{1,0:T(8,128)(2,1)}, u32[]{:S(2)}) copy-start(bf16[1280,256]{1,0:T(8,128)(2,1)} %param.23) | copy-start | bytes 1966084
Sparse Core Ops, SparseCore 0:
  25.6 33.7 all-reduce.4
  75.0 50.2 all-gather.4
  153.0 31.0 all-reduce.6
  206.6 20.8 reduce-scatter.4
  229.6 22.9 reduce-scatter.2
  278.4 31.0 all-reduce.8
where the time goes:
time: 319 us; the launch traced here: 318 us
  waiting for transfers between devices  131 us (41%)
  blocking collectives  107 us (34%)
  matrix products  41.5 us (13%)
  between operations  14.6 us (5%)
  other arithmetic  12 us (4%)
  local copies, waits for them, and re-layouts  11.5 us (4%)
    psum x1, blocking collectives, per_device(): lax.psum((query_part, key_part, value_part), 'mem')  39 us
    psum x1, waiting for transfers between devices, per_device(): lax.psum((query_part, key_part, value_part), 'mem')  32.1 us
    psum x1, waiting for transfers between devices, per_device(): lax.psum(jnp.dot(activated, down_weight, preferred_element_type=jnp.float...  31.2 us
    psum x1, waiting for transfers between devices, per_device(): lax.psum(jnp.dot(attended, output_weight, preferred_element_type=jnp.floa...  31.2 us
    all_gather x2, blocking collectives, combined_all(): pieces = jax.tree.map(lambda part: lax.all_gather(part, axis), value)  27.4 us
    reduce_scatter x1, waiting for transfers between devices, per_device(): lax.psum_scatter(gate_part, 'mem', scatter_dimension=0, tiled=True)  25.2 us
    all_gather x1, blocking collectives, per_device(): lax.all_gather((jax.nn.silu(gate_sum) * up_sum).astype(jnp.bfloat16), 'me...  15.2 us
    psum x1, blocking collectives, per_device(): squares = lax.psum(jnp.sum(residual * residual, axis=1), 'mem')  13.5 us
  transfers between devices with their start and end apart: 6, of which 5 were waited for; matrix products, arithmetic and copies ran while one was open for 4% of the time, Pallas kernels for 0%

commit v1 on v0

--- a/solution.py
+++ b/solution.py
@@ -182,8 +182,9 @@
     activated = lax.all_gather(
         (jax.nn.silu(gate_sum) * up_sum).astype(jnp.bfloat16), "mem", axis=0, tiled=True
     )
-    down_sum = lax.psum(
-        jnp.dot(activated, down_weight, preferred_element_type=jnp.float32), ("head", "width")
+    down_sum = jax.lax.psum(
+        jax.lax.psum(jnp.dot(activated, down_weight, preferred_element_type=jnp.float32), "width"),
+        "head",
     )
     return (middle_wide + down_sum).astype(jnp.bfloat16)
 

time: 319 us -> 330 us (1.034)
  waiting for transfers between devices: 131 us -> 142 us
    psum x1 -> x2, waiting for transfers between devices: 31.2 us -> 42.8 us  [the longest x1 25.5 us: per_device(): jax.lax.psum(jax.lax.psum(jnp.dot(activated, down_weight, preferred_eleme...]
  transfers between devices with their start and end apart: 6 -> 7, of which waited for: 5 -> 6; matrix products, arithmetic and copies ran while one was open for 4% -> 4% of each run, Pallas kernels for 0% -> 0%
where the time goes in v1:
time: 330 us
  waiting for transfers between devices  142 us (43%)
  blocking collectives  107 us (32%)
  matrix products  41.5 us (13%)
  between operations  14.6 us (4%)
  other arithmetic  12 us (4%)
  local copies, waits for them, and re-layouts  11.5 us (3%)
    psum x1, blocking collectives, per_device(): lax.psum((query_part, key_part, value_part), 'mem')  39 us
    psum x1, waiting for transfers between devices, per_device(): lax.psum((query_part, key_part, value_part), 'mem')  32.1 us
    psum x1, waiting for transfers between devices, per_device(): lax.psum(jnp.dot(attended, output_weight, preferred_element_type=jnp.floa...  31.2 us
    all_gather x2, blocking collectives, combined_all(): pieces = jax.tree.map(lambda part: lax.all_gather(part, axis), value)  27.4 us
    psum x1, waiting for transfers between devices, per_device(): jax.lax.psum(jax.lax.psum(jnp.dot(activated, down_weight, preferred_eleme...  25.5 us
    reduce_scatter x1, waiting for transfers between devices, per_device(): lax.psum_scatter(gate_part, 'mem', scatter_dimension=0, tiled=True)  25.2 us
    psum x1, waiting for transfers between devices, per_device(): jax.lax.psum(jnp.dot(activated, down_weight, preferred_element_type=jnp.f...  17.3 us
    all_gather x1, blocking collectives, per_device(): lax.all_gather((jax.nn.silu(gate_sum) * up_sum).astype(jnp.bfloat16), 'me...  15.2 us
  transfers between devices with their start and end apart: 7, of which 6 were waited for; matrix products, arithmetic and copies ran while one was open for 4% of the time, Pallas kernels for 0%

profile of v1, /device:TPU:0, one launch (start us, length us, event | category | flops | bytes accessed | tf_op | source)
XLA Modules:
  0.0 329.5 jit_solution(17447321221726007010)
XLA Ops:
  6.6 1.1 fusion.24
  7.7 13.5 %psum.56 = f32[32]{0:T(128)S(1)} all-reduce(f32[32]{0:T(128)S(1)} %fusion.24), channel_id=1, replica_groups=mesh['groups'=2,'mem'=4,'head'=2,'width'=2] {'mem'}, use_global_device_ids=true, to_apply=%region_2.0 | all-reduce | flops 32 | bytes 256 | tf_op jit(solution)/shard_map/psum | solution.py:79
  21.1 3.6 %convolution_bitcast_fusion.1 = f32[4,8,16,128]{3,1,2,0:T(8,128)S(1)} fusion(bf16[1280,2048]{1,0:T(8,128)(2,1)} %param.22, bf16[32,1280]{1,0:T(8,128)(2,1)} %param.20, f32[1280]{0:T(1024)} %param.21, f32[32]{0:T(128)S(1)} %add_rsqrt_fusion.3), kind=kOutput, calls=%fused_computation.38 | convolution fusion | flops 167936000 | bytes 5592192 | tf_op jit(solution)/shard_map/dot_general | solution.py:83
  24.7 0.8 copy.134
  27.3 32.1 %all-reduce.6.cloned.1.call-done = f32[32,16,128]{2,1,0:T(8,128)} async-done(((f32[32,16,128]{2,1,0:T(8,128)}), f32[32,16,128]{2,1,0:T(8,128)}) %all-reduce.6.cloned.1.call-update) | async-done | bytes 262160 | tf_op jit(solution)/shard_map/psum | solution.py:88
  59.5 1.1 multiply_reduce_fusion
  60.6 1.1 multiply_multiply_fusion
  62.2 12.0 %while.30 = (s32[]{:T(128)}, f32[32,2,8]{0,2,1:T(8,128)S(1)}, f32[32,2,8]{0,2,1:T(8,128)S(1)}, f32[32,2,8,128]{3,0,2,1:T(8,128)S(1)}, s32[]{:T(128)}, /*index=5*...) while((s32[]{:T(128)}, f32[32,2,8]{0,2,1:T(8,128)S(1)}, ...), condition=%wide.region_8.9_spmd.clone, body=%wide.region_5.8_spmd.clone.sunk | while | flops 274367744 | bytes 10269107 | solution.py:137
  62.3 2.0 constant_dynamic-slice_fusion.6
  66.3 1.9 constant_dynamic-slice_fusion.6
  70.3 1.9 constant_dynamic-slice_fusion.6
  75.5 39.0 %all-reduce = (bf16[32,256]{1,0:T(8,128)(2,1)S(1)}, f32[32,2,128]{2,0,1:T(8,128)S(1)}) all-reduce(f32[32,256]{1,0:T(8,128)S(1)} %fusion.45, f32[32,2,128]{2,0,1:T(8,128)S(1)} %bitcast.129), channel_id=1, replica_groups=mesh['groups'=2,'mem'=4,'head'=2,'width'=2] {'mem'}, use_global_device_ids=true, to_apply=%region_14.15 | all-reduce | flops 16384 | bytes 114688 | tf_op jit(solution)/shard_map/psum | solution.py:88
  114.9 14.1 %all-gather.1 = f32[128,2,8]{2,1,0:T(2,128)S(1)} all-gather(f32[32,2,8]{2,1,0:T(2,128)S(1)} %copy.92), channel_id=3, replica_groups=mesh['groups'=2,'mem'=4,'head'=2,'width'=2] {'mem'}, dimensions={0}, use_global_device_ids=true | all-gather | bytes 10240 | tf_op jit(solution)/shard_map/all_gather | solution.py:14
  129.0 13.3 %all-gather = f32[128,2,8]{2,1,0:T(2,128)S(1)} all-gather(f32[32,2,8]{2,1,0:T(2,128)S(1)} %copy.91), channel_id=2, replica_groups=mesh['groups'=2,'mem'=4,'head'=2,'width'=2] {'mem'}, dimensions={0}, use_global_device_ids=true | all-gather | bytes 10240 | tf_op jit(solution)/shard_map/all_gather | solution.py:14
  142.4 0.8 fusion.51
  143.6 1.0 slice.50
  144.8 1.2 slice.53
  146.0 1.7 while.29
  148.8 4.1 %fusion.32 = f32[32,1280]{1,0:T(8,128)} fusion(bf16[2048,1280]{1,0:T(8,128)(2,1)} %param.31, bf16[4,8,16,128]{3,2,1,0:T(8,128)(2,1)S(1)} %bitcast.122), kind=kOutput, calls=%fused_computation.66 | convolution fusion | flops 167772160 | bytes 5537792 | tf_op jit(solution)/shard_map/dot_general | solution.py:168
  152.9 31.2 %all-reduce.8.cloned.1.call-done = f32[32,1280]{1,0:T(8,128)} async-done(((f32[32,1280]{1,0:T(8,128)}), f32[32,1280]{1,0:T(8,128)}) %all-reduce.8.cloned.1.call-update) | async-done | bytes 163856 | tf_op jit(solution)/shard_map/psum | solution.py:167
  184.1 1.0 fusion.28
  185.1 11.7 %psum.61 = f32[32]{0:T(128)S(1)} all-reduce(f32[32]{0:T(128)S(1)} %get-tuple-element.230), channel_id=1, replica_groups=mesh['groups'=2,'mem'=4,'head'=2,'width'=2] {'mem'}, use_global_device_ids=true, to_apply=%region_18.19 | all-reduce | flops 32 | bytes 256 | tf_op jit(solution)/shard_map/psum | solution.py:172
  196.8 9.6 %fusion.37 = f32[32,6400]{1,0:T(8,128)} fusion(bf16[1280,6400]{1,0:T(8,128)(2,1)} %param.34, bf16[32,1280]{1,0:T(8,128)(2,1)S(1)} %get-tuple-element.231, f32[1280]{0:T(1024)S(1)} %copy-done.5, f32[32]{0:T(128)S(1)} %add_rsqrt_fusion.2), kind=kOutput, calls=%fused_computation.82 | convolution fusion | flops 524451840 | bytes 17290368 | tf_op jit(solution)/shard_map/dot_general | solution.py:177
  206.7 9.7 %fusion.39 = f32[32,6400]{1,0:T(8,128)} fusion(bf16[1280,6400]{1,0:T(8,128)(2,1)} %param.33, bf16[32,1280]{1,0:T(8,128)(2,1)S(1)} %get-tuple-element.231, f32[1280]{0:T(1024)S(1)} %copy-done.5, f32[32]{0:T(128)S(1)} %add_rsqrt_fusion.2), kind=kOutput, calls=%fused_computation.83 | convolution fusion | flops 524451840 | bytes 17290368 | tf_op jit(solution)/shard_map/dot_general | solution.py:176
  216.5 11.0 %reduce-scatter.5.cloned.1.call-done = f32[8,6400]{1,0:T(8,128)} async-done(((f32[32,6400]{1,0:T(8,128)}), f32[8,6400]{1,0:T(8,128)}) %reduce-scatter.5.cloned.1.call-update) | async-done | bytes 204816 | tf_op jit(solution)/shard_map/reduce_scatter | solution.py:180
  227.5 25.2 %reduce-scatter.3.cloned.1.call-done = f32[8,6400]{1,0:T(8,128)} async-done(((f32[32,6400]{1,0:T(8,128)}), f32[8,6400]{1,0:T(8,128)}) %reduce-scatter.3.cloned.1.call-update) | async-done | bytes 204816 | tf_op jit(solution)/shard_map/reduce_scatter | solution.py:179
  252.7 1.1 multiply_convert_fusion
  253.8 15.2 %all_gather.27 = bf16[32,6400]{1,0:T(8,128)(2,1)S(1)} all-gather(bf16[8,6400]{1,0:T(8,128)(2,1)S(1)} %multiply_convert_fusion), channel_id=1, replica_groups=mesh['groups'=2,'mem'=4,'head'=2,'width'=2] {'mem'}, dimensions={0}, use_global_device_ids=true | all-gather | bytes 512000 | tf_op jit(solution)/shard_map/all_gather | solution.py:182
  269.0 9.3 %fusion.52 = f32[32,1280]{1,0:T(8,128)} fusion(bf16[32,6400]{1,0:T(8,128)(2,1)S(1)} %all_gather.27, bf16[6400,1280]{1,0:T(8,128)(2,1)} %param.35), kind=kOutput, calls=%fused_computation.100 | convolution fusion | flops 524288000 | bytes 16957440 | tf_op jit(solution)/shard_map/dot_general | solution.py:186
  278.4 17.3 %all-reduce.10.cloned.1.call-done = f32[32,1280]{1,0:T(8,128)} async-done(((f32[32,1280]{1,0:T(8,128)}), f32[32,1280]{1,0:T(8,128)}) %all-reduce.10.cloned.1.call-update) | async-done | bytes 163856 | tf_op jit(solution)/shard_map/psum | solution.py:186
  295.7 25.5 %all-reduce.12.cloned.1.call-done = f32[32,1280]{1,0:T(8,128)} async-done(((f32[32,1280]{1,0:T(8,128)}), f32[32,1280]{1,0:T(8,128)}) %all-reduce.12.cloned.1.call-update) | async-done | bytes 163856 | tf_op jit(solution)/shard_map/psum | solution.py:185
  321.1 1.6 fusion.31
  (127 shorter events, 12.8 us)
Async XLA Ops:
  6.5 68.4 %copy-start = (bf16[1280,256]{1,0:T(8,128)(2,1)S(1)}, bf16[1280,256]{1,0:T(8,128)(2,1)}, u32[]{:S(2)}) copy-start(bf16[1280,256]{1,0:T(8,128)(2,1)} %param.23) | copy-start | bytes 1966084
  6.5 19.0 %copy-start.6 = (s32[8192]{0:T(1024)S(1)}, s32[8192]{0:T(1024)}, u32[]{:S(2)}) copy-start(s32[8192]{0:T(1024)} %param.29) | copy-start | bytes 98308
  6.5 19.8 %copy-start.10 = (s32[16]{0:T(128)S(1)}, s32[16]{0:T(128)}, u32[]{:S(2)}) copy-start(s32[16]{0:T(128)} %param.30) | copy-start | bytes 196
  6.5 54.0 %copy-start.8 = (f32[128]{0:T(128)S(1)}, f32[128]{0:T(128)}, u32[]{:S(2)}) copy-start(f32[128]{0:T(128)} %param.25) | copy-start | bytes 1540
  6.5 52.9 %all-reduce.6.cloned.1.call-start = ((), (), s32[]{:S(2)}) async-start(), calls=%async_computation.2 | async-start | bytes 524288 | tf_op jit(solution)/shard_map/psum | solution.py:88
  25.5 118.1 %all-gather.5.cloned.1.call-start = ((), (), s32[]{:S(2)}) async-start(), calls=%async_computation.8 | async-start | bytes 1310720 | tf_op jit(solution)/shard_map/all_gather | solution.py:14
  62.1 12.8 %copy-start.2 = (bf16[32,1280]{1,0:T(8,128)(2,1)S(1)}, bf16[32,1280]{1,0:T(8,128)(2,1)}, u32[]{:S(2)}) copy-start(bf16[32,1280]{1,0:T(8,128)(2,1)} %param.20) | copy-start | bytes 245764
  62.1 12.8 %copy-start.7 = (f32[1280]{0:T(1024)S(1)}, f32[1280]{0:T(1024)}, u32[]{:S(2)}) copy-start(f32[1280]{0:T(1024)} %param.21) | copy-start | bytes 15364
  62.1 13.1 %copy-start.4 = (bf16[1280,256]{1,0:T(8,128)(2,1)S(1)}, bf16[1280,256]{1,0:T(8,128)(2,1)}, u32[]{:S(2)}) copy-start(bf16[1280,256]{1,0:T(8,128)(2,1)} %param.24) | copy-start | bytes 1966084
  62.2 52.4 %copy-start.9 = (f32[128]{0:T(128)S(1)}, f32[128]{0:T(128)}, u32[]{:S(2)}) copy-start(f32[128]{0:T(128)} %param.26) | copy-start | bytes 1540
  74.1 0.7 copy-start.3
  74.9 109.2 %all-reduce.8.cloned.1.call-start = ((), (), s32[]{:S(2)}) async-start(), calls=%async_computation.3 | async-start | bytes 327680 | tf_op jit(solution)/shard_map/psum | solution.py:167
  147.6 49.2 %copy-start.5 = (f32[1280]{0:T(1024)S(1)}, f32[1280]{0:T(1024)}, u32[]{:S(2)}) copy-start(f32[1280]{0:T(1024)} %param.32) | copy-start | bytes 15364
  152.9 74.6 %reduce-scatter.5.cloned.1.call-start = ((), (), s32[]{:S(2)}) async-start(), calls=%async_computation.5 | async-start | bytes 1024000 | tf_op jit(solution)/shard_map/reduce_scatter | solution.py:180
  206.4 46.3 %reduce-scatter.3.cloned.1.call-start = ((), (), s32[]{:S(2)}) async-start(), calls=%async_computation.4 | async-start | bytes 1024000 | tf_op jit(solution)/shard_map/reduce_scatter | solution.py:179
  216.4 79.2 %all-reduce.10.cloned.1.call-start = ((), (), s32[]{:S(2)}) async-start(), calls=%async_computation.6 | async-start | bytes 327680 | tf_op jit(solution)/shard_map/psum | solution.py:186
  269.0 53.7 %copy-start.1 = (bf16[1280,256]{1,0:T(8,128)(2,1)S(1)}, bf16[1280,256]{1,0:T(8,128)(2,1)}, u32[]{:S(2)}) copy-start(bf16[1280,256]{1,0:T(8,128)(2,1)} %param.23) | copy-start | bytes 1966084
  278.3 42.8 %all-reduce.12.cloned.1.call-start = ((), (), s32[]{:S(2)}) async-start(), calls=%async_computation.7 | async-start | bytes 327680 | tf_op jit(solution)/shard_map/psum | solution.py:185
Sparse Core Ops, SparseCore 0:
  25.6 33.7 all-reduce.5
  75.0 50.2 all-gather.4
  153.0 31.0 all-reduce.7
  206.6 20.8 reduce-scatter.4
  229.6 22.9 reduce-scatter.2
  278.4 17.1 all-reduce.9
  297.9 23.1 all-reduce.11
